TPU v7x, 32 devices: a whole 2x2x4 slice. The times are simulated.
32 devices in a mesh: enc: 4 (over y, x), dec: 4 (over z), ret: 2 (over core).
Axes of the slice: x: 2, y: 2, z: 4, core: 2. Of those that a mesh axis runs over, the one named last changes fastest.
Arguments:
- enc_states: bfloat16 [8, 2, 256, 4096], P('enc', 'ret'), may hold values from -22 to 22
- kv_weight: bfloat16 [4096, 64, 128], P(None, 'dec'), may hold values from -1 to 1
- queries: bfloat16 [2, 128, 64, 64], P('ret', None, ('dec', 'enc')), may hold values from -47 to 47
- out_grad: bfloat16 [2, 128, 64, 64], P('ret', None, ('dec', 'enc')), may hold values from -6 to 6
- passage_order: int32 [2, 8], P('ret'), may hold values from 0 to 7, each once within a row
- passage_blocks: int32 [2, 8], P('ret'), may hold values from 1 to 2
- ret_tokens: bfloat16 [8, 2, 256, 768], P('enc', 'ret'), may hold values from -6 to 6
- ret_weight: bfloat16 [768, 768], replicated, may hold values from -0.21875 to 0.21875
- question_emb: float32 [2, 768], P('ret'), may hold values from -7 to 7
Outputs:
- kv_grad: bfloat16 [8, 2, 256, 64, 128], P('enc', 'ret', None, 'dec')
- kv_weight_grad: bfloat16 [4096, 64, 128], P(('enc', 'ret'), 'dec')
- ret_weight_grad: bfloat16 [768, 768], replicated
Inputs may be any that keep to these rules, and one draw needn't show every extreme that they name: `passage_order`: each row lists every passage of its group once; slots i * 8 to (i + 1) * 8 - 1 belong to question i of the group.
All inputs are finite; a program needn't handle non-finite values.
Results may differ from a plain program's by a relative error of at most 0.025.
Values may be sent and summed in bfloat16 or wider, within the bound.
A program may use at most 128 MiB of HBM per device.

v0:
```python
import functools
import math

import jax
import jax.numpy as jnp
from jax import lax
from jax.experimental import pallas as pl
from jax.experimental.pallas import tpu as pltpu
from jax.sharding import PartitionSpec as P

HEADS = 64
BLK = 128
PASS = 8


def gelu_grad(pre_act, upstream):
    return jax.vjp(jax.nn.gelu, pre_act)[1](upstream)[0]


def project_kernel(heads_here, x_ref, w_ref, out_ref, total, staged):
    step = pl.program_id(0)
    depth, heads, pair = w_ref.shape
    head_dim = pair // 2
    x = x_ref[...]
    staged[...] = w_ref[...].astype(jnp.float32).reshape(depth * heads, pair)
    for first in range(0, heads, 2):
        w_two = jnp.concatenate(
            [
                staged[pl.ds(first + k, depth, stride=heads), :].astype(jnp.bfloat16)
                for k in range(2)
            ],
            axis=-1,
        )
        part = jnp.dot(x, w_two, preferred_element_type=jnp.float32)
        cols = slice(first * pair, (first + 2) * pair)

        @pl.when(step == 0)
        def _():
            total[:, cols] = part

        @pl.when(step > 0)
        def _():
            total[:, cols] += part

    @pl.when(step == pl.num_programs(0) - 1)
    def _():
        for h in range(heads):
            dest, own = h // heads_here, h % heads_here
            wide = total[:, h * pair : (h + 1) * pair]
            high = wide.astype(jnp.bfloat16)
            low = (wide - high.astype(jnp.float32)).astype(jnp.bfloat16)
            out_ref[dest, :, own * pair : (own + 1) * pair] = high
            start = heads_here * pair + own * head_dim
            out_ref[dest, :, start : start + head_dim] = low[:, :head_dim]


def project(tok_rows, kv_weight, shards):
    rows, width = tok_rows.shape
    _, heads, pair = kv_weight.shape
    heads_here = heads // shards
    depth = min(512, width)
    cols = heads_here * (pair + pair // 2)
    return pl.pallas_call(
        functools.partial(project_kernel, heads_here),
        grid=(width // depth,),
        in_specs=[
            pl.BlockSpec((rows, depth), lambda i: (0, i)),
            pl.BlockSpec((depth, heads, pair), lambda i: (i, 0, 0)),
        ],
        out_specs=pl.BlockSpec((shards, rows, cols), lambda i: (0, 0, 0)),
        out_shape=jax.ShapeDtypeStruct((shards, rows, cols), jnp.bfloat16),
        scratch_shapes=[
            pltpu.VMEM((rows, heads * pair), jnp.float32),
            pltpu.VMEM((depth * heads, pair), jnp.float32),
        ],
        cost_estimate=pl.CostEstimate(
            flops=2 * rows * width * heads * pair,
            bytes_accessed=2 * (rows * width + width * heads * pair + shards * rows * cols),
            transcendentals=0,
        ),
        name="project",
    )(tok_rows, kv_weight)


def attend_kernel(scale, x_ref, kv_ref, live_ref, grad_ref, mass_ref):
    heads = x_ref.shape[1]
    rows = x_ref.shape[2] // 2
    pair = x_ref.shape[3]
    head_dim = pair // 2
    last = (((1,), (1,)), ((), ()))
    live = live_ref[0] > 0.0
    mass = None
    for h in range(heads):
        x = x_ref[0, h]
        both = kv_ref[0, :, h * pair : (h + 1) * pair]
        start = heads * pair + h * head_dim
        low = kv_ref[0, :, start : start + head_dim]
        s = lax.dot_general(x, both, last, preferred_element_type=jnp.float32)
        s_low = lax.dot_general(
            x[:rows, :head_dim], low, last, preferred_element_type=jnp.float32
        )
        scores = jnp.where(live, (s[:rows] + s_low) * scale, -1e30)
        top = jnp.max(scores, axis=-1, keepdims=True)
        expo = jnp.where(live, jnp.exp(scores - top), 0.0)
        probs = expo / jnp.sum(expo, axis=-1, keepdims=True)
        probs_low = probs.astype(jnp.bfloat16)
        prob_grad = s[rows:]
        row_dot = jnp.sum(probs_low.astype(jnp.float32) * prob_grad, axis=-1, keepdims=True)
        score_grad = (probs * (prob_grad - row_dot) * scale).astype(jnp.bfloat16)
        y = jnp.concatenate([score_grad, probs_low], axis=0)
        pair_grad = lax.dot_general(
            y, x, (((0,), (0,)), ((), ())), preferred_element_type=jnp.float32
        )
        grad_ref[0, :, h * pair : (h + 1) * pair] = pair_grad.astype(jnp.bfloat16)
        part = jnp.sum(probs, axis=0, keepdims=True)
        mass = part if mass is None else mass + part
    mass_ref[0] = mass


def attend(x, kv, live, scale):
    count, heads, double_rows, pair = x.shape
    keys, cols = kv.shape[1:]
    return pl.pallas_call(
        functools.partial(attend_kernel, scale),
        grid=(count,),
        in_specs=[
            pl.BlockSpec((1, heads, double_rows, pair), lambda q: (q, 0, 0, 0)),
            pl.BlockSpec((1, keys, cols), lambda q: (q, 0, 0)),
            pl.BlockSpec((1, 1, keys), lambda q: (q, 0, 0)),
        ],
        out_specs=[
            pl.BlockSpec((1, keys, heads * pair), lambda q: (q, 0, 0)),
            pl.BlockSpec((1, 1, keys), lambda q: (q, 0, 0)),
        ],
        out_shape=[
            jax.ShapeDtypeStruct((count, keys, heads * pair), jnp.bfloat16),
            jax.ShapeDtypeStruct((count, 1, keys), jnp.float32),
        ],
        cost_estimate=pl.CostEstimate(
            flops=5 * count * heads * double_rows * keys * pair,
            bytes_accessed=2 * count * keys * (cols + heads * pair),
            transcendentals=count * heads * double_rows * keys // 2,
        ),
        name="attend",
    )(x, kv, live)


def spread_kernel(where_ref, piece_ref, out_ref, staged):
    shards = piece_ref.shape[0]
    rows, heads, pair = out_ref.shape
    heads_here = heads // shards
    for j in range(shards):
        piece = piece_ref[where_ref[j]].astype(jnp.float32)
        for h in range(heads_here):
            staged[pl.ds(j * heads_here + h, rows, stride=heads), :] = piece[
                :, h * pair : (h + 1) * pair
            ]
    out_ref[...] = staged[...].reshape(rows, heads, pair).astype(out_ref.dtype)


def spread(pieces, where, pair):
    shards, rows, cols = pieces.shape
    heads = shards * cols // pair
    step = min(128, rows)
    return pl.pallas_call(
        spread_kernel,
        grid_spec=pltpu.PrefetchScalarGridSpec(
            num_scalar_prefetch=1,
            grid=(rows // step,),
            in_specs=[pl.BlockSpec((shards, step, cols), lambda i, w: (0, i, 0))],
            out_specs=pl.BlockSpec((step, heads, pair), lambda i, w: (i, 0, 0)),
            scratch_shapes=[pltpu.VMEM((step * heads, pair), jnp.float32)],
        ),
        out_shape=jax.ShapeDtypeStruct((rows, heads, pair), jnp.bfloat16),
        cost_estimate=pl.CostEstimate(
            flops=0, bytes_accessed=4 * shards * rows * cols, transcendentals=0
        ),
        name="spread",
    )(where, pieces)


def wedge(left, right):
    return lax.dot_general(
        left, right, (((0,), (0,)), ((), ())), preferred_element_type=jnp.float32
    )


def on_device(
    enc_states,
    kv_weight,
    queries,
    out_grad,
    passage_order,
    passage_blocks,
    ret_tokens,
    ret_weight,
    question_emb,
):
    pass_dev = enc_states.shape[0]
    slot_len = enc_states.shape[2]
    width = enc_states.shape[3]
    pair_width = kv_weight.shape[2]
    heads_dec = kv_weight.shape[1]
    head_dim = pair_width // 2
    n_enc = lax.axis_size("enc")
    n_ret = lax.axis_size("ret")
    enc_rank = lax.axis_index("enc")
    dec_rank = lax.axis_index("dec")
    ret_rank = lax.axis_index("ret")
    order_row = passage_order[0]
    blocks_row = passage_blocks[0]
    group_pass = order_row.shape[0]
    question_count = queries.shape[0]
    query_len = queries.shape[1]
    heads_here = queries.shape[2]
    highest = lax.Precision.HIGHEST
    rows_dev = pass_dev * slot_len
    key_count = PASS * slot_len
    tok_rows = enc_states.reshape(rows_dev, width)

    rows_out = width // (n_enc * n_ret)
    rows_group = group_pass * slot_len
    split_cols = tok_rows.reshape(rows_dev, n_enc, n_ret, rows_out)

    def columns_of(rank):
        block = lax.dynamic_index_in_dim(split_cols, rank, axis=2, keepdims=False)
        block = jnp.transpose(block, (1, 0, 2))
        return lax.all_to_all(block, "enc", split_axis=0, concat_axis=0, tiled=True).reshape(
            rows_group, rows_out
        )

    own_cols = columns_of(ret_rank)

    sent = project(tok_rows, kv_weight, n_enc)
    kv = lax.all_to_all(sent, "enc", split_axis=0, concat_axis=0, tiled=True)
    cols = kv.shape[2]
    other_cols = [columns_of((ret_rank + shift) % n_ret) for shift in range(1, n_ret)]

    positions = jnp.arange(slot_len, dtype=jnp.int32)
    live_pass = (positions[None, :] < BLK * blocks_row[:, None]).astype(jnp.float32)
    chosen = order_row.reshape(question_count, PASS)
    if question_count == 1:
        kv = kv.reshape(1, key_count, cols)
        live = live_pass.reshape(1, 1, key_count)
    else:
        kv = kv.reshape(group_pass, slot_len, cols)[chosen].reshape(
            question_count, key_count, cols
        )
        live = live_pass[chosen].reshape(question_count, 1, key_count)
    query_t = jnp.transpose(queries, (0, 2, 1, 3))
    grad_t = jnp.transpose(out_grad, (0, 2, 1, 3))
    zero = jnp.zeros_like(query_t)
    x = jnp.concatenate(
        [
            jnp.concatenate([query_t, zero], axis=-1),
            jnp.concatenate([zero, grad_t], axis=-1),
        ],
        axis=2,
    )
    pair_grad, mass_keys = attend(x, kv, live, 1.0 / math.sqrt(head_dim))
    mass_part = mass_keys.reshape(question_count, PASS, slot_len).sum(axis=-1) / (
        HEADS * query_len
    )
    if question_count == 1:
        own_grad = pair_grad.reshape(rows_group, heads_here * pair_width)
        mass_part = mass_part[0][order_row][None]
    else:
        own_grad = (
            jnp.zeros((group_pass, slot_len, heads_here * pair_width), jnp.bfloat16)
            .at[order_row]
            .set(pair_grad.reshape(group_pass, slot_len, heads_here * pair_width))
            .reshape(rows_group, heads_here * pair_width)
        )

    own_blocks = lax.dynamic_slice_in_dim(blocks_row, enc_rank * pass_dev, pass_dev)
    ret_rows = ret_tokens.reshape(pass_dev * slot_len, ret_tokens.shape[3])
    ret_width = ret_rows.shape[1]
    pre_act = jnp.dot(ret_rows, ret_weight, preferred_element_type=jnp.float32).reshape(
        pass_dev, slot_len, ret_width
    )
    hidden = jax.nn.gelu(pre_act)
    own_live = positions[None, :] < BLK * own_blocks[:, None]
    own_length = (BLK * own_blocks).astype(jnp.float32)
    embed_own = jnp.sum(jnp.where(own_live[..., None], hidden, 0.0), axis=1) / own_length[:, None]
    owner_map = (
        order_row[:, None] == enc_rank * pass_dev + jnp.arange(pass_dev, dtype=jnp.int32)[None, :]
    ).astype(jnp.float32)
    slot_embed = jnp.dot(owner_map, embed_own, precision=highest)
    emb_rep = jnp.repeat(question_emb, PASS, axis=0)
    score_part = jnp.sum(emb_rep * slot_embed, axis=-1) * (dec_rank == 0).astype(jnp.float32)
    passage_mass, ret_scores = lax.psum(
        (mass_part, score_part.reshape(question_count, PASS)), ("enc", "dec")
    )
    own_grad, passage_mass, ret_scores = lax.optimization_barrier(
        (own_grad, passage_mass, ret_scores)
    )

    half = rows_group // 2
    if n_enc == 4:
        flip = [[(i, i ^ bit) for i in range(n_enc)] for bit in (1, 2)]
        tops, bottoms = own_grad[:half], own_grad[half:]
        one_top = lax.ppermute(tops, "enc", flip[0])
        two_bottom = lax.ppermute(bottoms, "enc", flip[1])
        one_bottom = lax.ppermute(bottoms, "enc", flip[0])
        two_top = lax.ppermute(tops, "enc", flip[1])
        three_top = lax.ppermute(one_top, "enc", flip[1])
        three_bottom = lax.ppermute(two_bottom, "enc", flip[0])
        parts = [
            (tops, bottoms),
            (one_top, one_bottom),
            (two_top, two_bottom),
            (three_top, three_bottom),
        ]
        where = jnp.arange(n_enc, dtype=jnp.int32) ^ enc_rank
    else:
        gathered = lax.all_gather(own_grad, "enc", axis=0, tiled=False)
        parts = [(gathered[k][:half], gathered[k][half:]) for k in range(n_enc)]
        where = jnp.arange(n_enc, dtype=jnp.int32)

    own_sums = []
    for top, bottom in parts:
        piece = wedge(own_cols[:half], top) + wedge(own_cols[half:], bottom)
        for shift in range(1, n_ret):
            left = other_cols[shift - 1]
            away = (wedge(left[:half], top) + wedge(left[half:], bottom)).astype(jnp.bfloat16)
            got = lax.ppermute(away, "ret", [(i, (i + shift) % n_ret) for i in range(n_ret)])
            piece = piece + got.astype(jnp.float32)
        own_sums.append(piece.astype(jnp.bfloat16))
    weight_total = spread(jnp.stack(own_sums), where, pair_width)

    first_row = enc_rank * rows_dev
    mine = []
    for top, bottom in parts:
        in_top = lax.dynamic_slice_in_dim(top, jnp.minimum(first_row, half - rows_dev), rows_dev)
        in_bottom = lax.dynamic_slice_in_dim(
            bottom, jnp.maximum(first_row - half, 0), rows_dev
        )
        mine.append(jnp.where(first_row < half, in_top, in_bottom))
    kv_grad = spread(jnp.stack(mine), where, pair_width).reshape(
        pass_dev, 1, slot_len, heads_dec, pair_width
    )

    top_score = jnp.max(ret_scores, axis=-1, keepdims=True)
    expo_score = jnp.exp(ret_scores - top_score)
    score_gap = expo_score / jnp.sum(expo_score, axis=-1, keepdims=True) - passage_mass
    gap_rows = score_gap.reshape(-1, 1) * emb_rep
    embed_grad = jnp.dot(jnp.transpose(owner_map), gap_rows, precision=highest)
    hidden_grad = jnp.where(
        own_live[..., None], (embed_grad / own_length[:, None])[:, None, :], 0.0
    )
    pre_grad = gelu_grad(pre_act, hidden_grad).astype(jnp.bfloat16)
    ret_part_grad = wedge(ret_rows, pre_grad.reshape(-1, ret_width))
    ret_weight_grad = lax.psum(ret_part_grad.astype(jnp.bfloat16), ("enc", "ret"))
    return (kv_grad, weight_total, ret_weight_grad)


def solution(mesh):
    return jax.shard_map(
        on_device,
        mesh=mesh,
        in_specs=(
            P("enc", "ret", None, None),
            P(None, "dec", None),
            P("ret", None, ("dec", "enc"), None),
            P("ret", None, ("dec", "enc"), None),
            P("ret", None),
            P("ret", None),
            P("enc", "ret", None, None),
            P(),
            P("ret", None),
        ),
        out_specs=(P("enc", "ret", None, "dec", None), P(("enc", "ret"), "dec", None), P()),
        check_vma=False,
    )
```

profile of v0, /device:TPU:0, one launch (start us, length us, event | category | flops | bytes accessed | tf_op | source)
XLA Modules:
  0.0 336.7 jit_solution(18155343100376912628)
XLA Ops:
  7.2 7.9 %reshape_reshape.3 = bf16[512,4,2,512]{3,2,1,0:T(2,128)(2,1)} reshape(bf16[2,1,256,4096]{3,2,1,0:T(8,128)(2,1)} %param.9) | data formatting | bytes 8388608 | tf_op jit(solution)/shard_map/reshape;reshape | solution.py:223
  15.1 11.2 %constant_dynamic-slice_fusion.1 = (bf16[512,4,1,512]{3,2,1,0:T(2,128)(2,1)S(1)}, bf16[512,4,1,512]{3,2,1,0:T(2,128)(2,1)}) fusion(bf16[512,4,2,512]{3,2,1,0:T(2,128)(2,1)} %reshape_reshape.3, s32[]{:T(128)S(6)} %select_n.76, s32[]{:T(128)S(6)} %select_n.74), kind=kLoop, calls=%fused_computation.72 | loop fusion | bytes 8388616 | tf_op jit(solution)/shard_map/jit(dynamic_index_in_dim)/dynamic_slice | solution.py:226
  26.3 2.5 copy.28
  28.8 5.2 %all-to-all-start.2 = ((bf16[4,512,512]{2,1,0:T(8,128)(2,1)}), bf16[4,512,512]{2,1,0:T(8,128)(2,1)S(1)}, u32[]{:S(2)}, u32[]{:S(2)}) async-start(bf16[4,512,512]{2,1,0:T(8,128)(2,1)} %bitcast.97), calls=%async_computation.2 | async-start | bytes 4194304 | tf_op jit(solution)/shard_map/all_to_all | solution.py:228
  33.9 4.7 %copy.29 = bf16[512,4,1,512]{3,0,2,1:T(8,128)(2,1)} copy(bf16[512,4,1,512]{3,2,1,0:T(2,128)(2,1)} %get-tuple-element.27) | data formatting | bytes 4194304 | tf_op jit(solution)/shard_map/jit(dynamic_index_in_dim)/dynamic_slice | solution.py:226
  38.6 20.2 %all-to-all-done.2 = bf16[4,512,512]{2,1,0:T(8,128)(2,1)S(1)} async-done(((bf16[4,512,512]{2,1,0:T(8,128)(2,1)}), bf16[4,512,512]{2,1,0:T(8,128)(2,1)S(1)}, u32[]{:S(2)}, u32[]{:S(2)}) %all-to-all-start.2) | async-done | bytes 2097184 | tf_op jit(solution)/shard_map/all_to_all | solution.py:228
  58.8 4.6 %all-to-all-start.1 = ((bf16[4,512,512]{2,1,0:T(8,128)(2,1)}), bf16[4,512,512]{2,1,0:T(8,128)(2,1)}, u32[]{:S(2)}, u32[]{:S(2)}) async-start(bf16[4,512,512]{2,1,0:T(8,128)(2,1)} %bitcast.98), calls=%async_computation.1 | async-start | bytes 4194304 | tf_op jit(solution)/shard_map/all_to_all | solution.py:228
  63.4 39.6 %project.1 = bf16[4,512,768]{2,1,0:T(8,128)(2,1)} custom-call(bf16[512,4096]{1,0:T(8,128)(2,1)} %bitcast.99, bf16[4096,16,128]{2,1,0:T(8,128)(2,1)} %w_ref.1), custom_call_target="tpu_custom_call" | custom-call | flops 8589934592 | bytes 24117248 | tf_op jit(solution)/shard_map/project/pallas_call | solution.py:63
  103.1 4.8 %all-to-all-start = ((bf16[4,512,768]{2,1,0:T(8,128)(2,1)}), bf16[4,512,768]{2,1,0:T(8,128)(2,1)}, u32[]{:S(2)}, u32[]{:S(2)}) async-start(bf16[4,512,768]{2,1,0:T(8,128)(2,1)} %project.1), calls=%async_computation | async-start | bytes 6291456 | tf_op jit(solution)/shard_map/all_to_all | solution.py:235
  108.3 1.0 copy.21
  111.3 3.2 select_reduce_fusion
  114.9 0.8 fusion.31.x_ref
  115.7 1.4 fusion.59
  117.2 2.7 fusion.60
  119.9 23.7 %all-to-all-done = bf16[4,512,768]{2,1,0:T(8,128)(2,1)} async-done(((bf16[4,512,768]{2,1,0:T(8,128)(2,1)}), bf16[4,512,768]{2,1,0:T(8,128)(2,1)}, u32[]{:S(2)}, u32[]{:S(2)}) %all-to-all-start) | async-done | bytes 3145760 | tf_op jit(solution)/shard_map/all_to_all | solution.py:235
  143.6 9.6 %attend.1 = (bf16[1,2048,512]{2,1,0:T(8,128)(2,1)}, f32[1,1,2048]{2,1,0:T(1,128)}) custom-call(bf16[1,4,256,128]{3,2,1,0:T(8,128)(2,1)} %fusion.31.x_ref, bf16[1,2048,768]{2,1,0:T(8,128)(2,1)} %bitcast.3.kv_ref, f32[1,1,2048]{2,1,0:T(1,128)} %reshape.182.live_ref), custom_call_target="tpu_custom_call" | custom-call | flops 1342177280 | bytes 5242880 | tf_op jit(solution)/shard_map/attend/pallas_call | solution.py:123
  153.6 1.4 reduce.7
  155.8 41.8 %all-reduce.2 = (f32[1,8]{1,0:T(1,128)S(1)}, f32[1,8]{1,0:T(1,128)S(1)}) all-reduce(f32[1,8]{1,0:T(1,128)S(1)} %bitcast.125, f32[1,8]{1,0:T(1,128)S(1)} %multiply_bitcast_fusion), channel_id=1, replica_groups=mesh['enc'=4,'dec'=4,'ret'=2] {'enc','dec'}, use_global_device_ids=true, to_apply=%region_1.2 | all-reduce | flops 16 | bytes 128 | tf_op jit(solution)/shard_map/psum | solution.py:291
  197.6 1.8 fusion.61
  199.5 1.5 collective-permute-start.3
  201.0 1.9 collective-permute-start
  204.7 1.5 fusion.14
  206.9 1.4 fusion.48
  208.3 1.3 fusion.47
  209.9 2.6 fusion.6
  212.5 1.8 fusion.10
  214.4 2.1 fusion.55
  216.8 1.0 copy-done.6
  217.8 2.6 fusion.28
  220.4 51.5 %all-reduce.5.cloned.1.call-done = bf16[768,768]{0,1:T(8,128)(2,1)} async-done(((bf16[768,768]{0,1:T(8,128)(2,1)}), bf16[768,768]{0,1:T(8,128)(2,1)}) %all-reduce.5.cloned.1.call-update) | async-done | bytes 1179664 | tf_op jit(solution)/shard_map/psum | solution.py:353
  272.0 2.4 copy.25
  274.3 2.4 fusion.63
  276.7 2.0 fusion.15
  278.9 2.0 fusion.65
  280.9 2.0 fusion.16
  283.5 1.9 fusion.62
  286.6 2.0 fusion.64
  288.5 1.6 select_bitcast_fusion.2
  290.1 1.5 select_bitcast_fusion.1
  291.6 2.8 fusion.23
  294.4 2.8 fusion.22
  297.1 13.6 %collective-permute-done.5 = bf16[1024,512]{1,0:T(8,128)(2,1)S(1)} collective-permute-done((bf16[1024,512]{1,0:T(8,128)(2,1)}, bf16[1024,512]{1,0:T(8,128)(2,1)S(1)}, u32[]{:S(2)}, u32[]{:S(2)}) %collective-permute-start.5) | collective-permute-done | bytes 1048608 | tf_op jit(solution)/shard_map/ppermute | solution.py:307
  311.5 1.5 fusion.17
  313.4 1.6 pad_maximum_fusion.piece_ref
  314.9 5.2 %spread.2 = bf16[512,16,128]{2,1,0:T(8,128)(2,1)} custom-call(s32[4]{0:T(128)} %iota_xor_fusion.where_ref, bf16[4,512,512]{2,1,0:T(8,128)(2,1)} %pad_maximum_fusion.piece_ref), custom_call_target="tpu_custom_call" | custom-call | bytes 4194304 | tf_op jit(solution)/shard_map/spread/pallas_call | solution.py:165
  321.3 1.8 fusion.21
  323.2 1.6 pad_maximum_fusion.1.piece_ref
  324.8 5.0 %spread.3 = bf16[512,16,128]{2,1,0:T(8,128)(2,1)} custom-call(s32[4]{0:T(128)} %iota_xor_fusion.where_ref, bf16[4,512,512]{2,1,0:T(8,128)(2,1)} %pad_maximum_fusion.1.piece_ref), custom_call_target="tpu_custom_call" | custom-call | bytes 4194304 | tf_op jit(solution)/shard_map/spread/pallas_call | solution.py:165
  (102 shorter events, 11.2 us)
Async XLA Ops:
  7.2 104.2 %copy-start = (bf16[768,768]{1,0:T(8,128)(2,1)S(1)}, bf16[768,768]{1,0:T(8,128)(2,1)}, u32[]{:S(2)}) copy-start(bf16[768,768]{1,0:T(8,128)(2,1)} %param.16) | copy-start | bytes 3538948
  28.8 30.1 %all-to-all-start.2 = ((bf16[4,512,512]{2,1,0:T(8,128)(2,1)}), bf16[4,512,512]{2,1,0:T(8,128)(2,1)S(1)}, u32[]{:S(2)}, u32[]{:S(2)}) async-start(bf16[4,512,512]{2,1,0:T(8,128)(2,1)} %bitcast.97), calls=%async_computation.2 | async-start | bytes 4194304 | tf_op jit(solution)/shard_map/all_to_all | solution.py:228
  58.8 4.6 %copy-start.22 = (s32[1,8]{1,0:T(1,128)S(1)}, s32[1,8]{1,0:T(1,128)}, u32[]{:S(2)}) copy-start(s32[1,8]{1,0:T(1,128)} %param.14) | copy-start | bytes 100
  58.8 44.3 %all-to-all-start.1 = ((bf16[4,512,512]{2,1,0:T(8,128)(2,1)}), bf16[4,512,512]{2,1,0:T(8,128)(2,1)}, u32[]{:S(2)}, u32[]{:S(2)}) async-start(bf16[4,512,512]{2,1,0:T(8,128)(2,1)} %bitcast.98), calls=%async_computation.1 | async-start | bytes 4194304 | tf_op jit(solution)/shard_map/all_to_all | solution.py:228
  103.1 5.1 %copy-start.20 = (bf16[1,128,4,64]{1,3,2,0:T(8,128)(2,1)S(1)}, bf16[1,128,4,64]{1,3,2,0:T(8,128)(2,1)}, u32[]{:S(2)}) copy-start(bf16[1,128,4,64]{1,3,2,0:T(8,128)(2,1)} %param.11) | copy-start | bytes 196612
  103.1 6.8 %copy-start.21 = (f32[1,768]{1,0:T(1,128)S(1)}, f32[1,768]{1,0:T(1,128)}, u32[]{:S(2)}) copy-start(f32[1,768]{1,0:T(1,128)} %param.17) | copy-start | bytes 9220
  103.1 40.5 %all-to-all-start = ((bf16[4,512,768]{2,1,0:T(8,128)(2,1)}), bf16[4,512,768]{2,1,0:T(8,128)(2,1)}, u32[]{:S(2)}, u32[]{:S(2)}) async-start(bf16[4,512,768]{2,1,0:T(8,128)(2,1)} %project.1), calls=%async_computation | async-start | bytes 6291456 | tf_op jit(solution)/shard_map/all_to_all | solution.py:235
  107.9 164.1 %all-reduce.5.cloned.1.call-start = ((), (), s32[]{:S(2)}) async-start(), calls=%async_computation.3 | async-start | bytes 2359296 | tf_op jit(solution)/shard_map/psum | solution.py:353
  109.9 4.7 %copy-start.27 = (s32[2]{0:T(128)}, s32[2]{0:T(128)S(1)}, u32[]{:S(2)}) copy-start(s32[2]{0:T(128)S(1)} %iota_add_fusion) | copy-start | bytes 28
  110.6 4.0 %copy-start.23 = (f32[2]{0:T(128)}, f32[2]{0:T(128)S(1)}, u32[]{:S(2)}) copy-start(f32[2]{0:T(128)S(1)} %get-tuple-element.24) | copy-start | bytes 28
  111.3 3.3 copy-start.26
  119.9 94.5 %copy-start.4 = (bf16[2,512,512]{2,1,0:T(8,128)(2,1)}, bf16[2,512,512]{2,1,0:T(8,128)(2,1)S(1)}, u32[]{:S(2)}) copy-start(bf16[2,512,512]{2,1,0:T(8,128)(2,1)S(1)} %get-tuple-element.30) | copy-start | bytes 3145732
  197.6 6.0 %copy-start.2 = (bf16[1,2048,512]{2,1,0:T(8,128)(2,1)S(1)}, bf16[1,2048,512]{2,1,0:T(8,128)(2,1)}, u32[]{:S(2)}) copy-start(bf16[1,2048,512]{2,1,0:T(8,128)(2,1)} %get-tuple-element.8) | copy-start | bytes 6291460
  197.6 6.0 %copy-start.9 = (bf16[2,512,512]{2,1,0:T(8,128)(2,1)S(1)}, bf16[2,512,512]{2,1,0:T(8,128)(2,1)}, u32[]{:S(2)}) copy-start(bf16[2,512,512]{2,1,0:T(8,128)(2,1)} %get-tuple-element.28) | copy-start | bytes 3145732
  199.4 75.0 %collective-permute-start.1 = (bf16[1024,512]{1,0:T(8,128)(2,1)S(1)}, bf16[1024,512]{1,0:T(8,128)(2,1)}, u32[]{:S(2)}, u32[]{:S(2)}) collective-permute-start(bf16[1024,512]{1,0:T(8,128)(2,1)S(1)} %get-tuple-element.33), channel_id=1, source_target_pairs={{0,8},{8,0},{16,24},{24,16},{1,9},{9,1},{17,25},{25,17},{2,10},{10... | collective-permute-start | bytes 3145736 | tf_op jit(solution)/shard_map/ppermute | solution.py:304
  199.5 79.4 %collective-permute-start.3 = (bf16[1024,512]{1,0:T(8,128)(2,1)S(1)}, bf16[1024,512]{1,0:T(8,128)(2,1)}, u32[]{:S(2)}, u32[]{:S(2)}) collective-permute-start(bf16[1024,512]{1,0:T(8,128)(2,1)S(1)} %get-tuple-element.33), channel_id=1, source_target_pairs={{0,16},{8,24},{16,0},{24,8},{1,17},{9,25},{17,1},{25,9},{2,18},{10... | collective-permute-start | bytes 3145736 | tf_op jit(solution)/shard_map/ppermute | solution.py:303
  201.0 75.7 %collective-permute-start = (bf16[1024,512]{1,0:T(8,128)(2,1)S(1)}, bf16[1024,512]{1,0:T(8,128)(2,1)}, u32[]{:S(2)}, u32[]{:S(2)}) collective-permute-start(bf16[1024,512]{1,0:T(8,128)(2,1)S(1)} %get-tuple-element.32), channel_id=1, source_target_pairs={{0,8},{8,0},{16,24},{24,16},{1,9},{9,1},{17,25},{25,17},{2,10},{10... | collective-permute-start | bytes 3145736 | tf_op jit(solution)/shard_map/ppermute | solution.py:302
  202.9 77.9 %collective-permute-start.2 = (bf16[1024,512]{1,0:T(8,128)(2,1)S(1)}, bf16[1024,512]{1,0:T(8,128)(2,1)}, u32[]{:S(2)}, u32[]{:S(2)}) collective-permute-start(bf16[1024,512]{1,0:T(8,128)(2,1)S(1)} %get-tuple-element.32), channel_id=1, source_target_pairs={{0,16},{8,24},{16,0},{24,8},{1,17},{9,25},{17,1},{25,9},{2,18},{10... | collective-permute-start | bytes 3145736 | tf_op jit(solution)/shard_map/ppermute | solution.py:305
  203.5 1.2 copy-start.11
  204.7 4.9 %copy-start.24 = (f32[2]{0:T(128)S(1)}, f32[2]{0:T(128)}, u32[]{:S(2)}) copy-start(f32[2]{0:T(128)} %copy-done.23) | copy-start | bytes 28
  204.7 4.9 %copy-start.28 = (s32[2]{0:T(128)S(1)}, s32[2]{0:T(128)}, u32[]{:S(2)}) copy-start(s32[2]{0:T(128)} %copy-done.27) | copy-start | bytes 28
  206.3 10.5 %collective-permute-start.6 = (bf16[512,512]{1,0:T(8,128)(2,1)}, bf16[512,512]{1,0:T(8,128)(2,1)}, u32[]{:S(2)}, u32[]{:S(2)}) collective-permute-start(bf16[512,512]{1,0:T(8,128)(2,1)} %fusion.14), channel_id=1, source_target_pairs={{0,1},{1,0},{2,3},{3,2},{4,5},{5,4},{6,7},{7,6},{8,9},{9,8},{10,11... | collective-permute-start | bytes 1572872 | tf_op jit(solution)/shard_map/ppermute | solution.py:326
  206.9 5.6 %copy-start.25 = (bf16[2,1,256,768]{3,2,1,0:T(8,128)(2,1)S(1)}, bf16[2,1,256,768]{3,2,1,0:T(8,128)(2,1)}, u32[]{:S(2)}) copy-start(bf16[2,1,256,768]{3,2,1,0:T(8,128)(2,1)} %param.15) | copy-start | bytes 2359300
  214.4 2.4 copy-start.3
  216.5 1.3 copy-start.6
  274.3 2.4 copy-start.10
  276.7 2.2 copy-start.12
  278.8 12.8 %collective-permute-start.7 = (bf16[512,512]{1,0:T(8,128)(2,1)S(1)}, bf16[512,512]{1,0:T(8,128)(2,1)S(1)}, u32[]{:S(2)}, u32[]{:S(2)}) collective-permute-start(bf16[512,512]{1,0:T(8,128)(2,1)S(1)} %fusion.15), channel_id=1, source_target_pairs={{0,1},{1,0},{2,3},{3,2},{4,5},{5,4},{6,7},{7,6},{8,9},{9,8},{10,11... | collective-permute-start | bytes 1572872 | tf_op jit(solution)/shard_map/ppermute | solution.py:326
  280.8 2.6 copy-start.7
  282.9 11.5 %collective-permute-start.8 = (bf16[512,512]{1,0:T(8,128)(2,1)S(1)}, bf16[512,512]{1,0:T(8,128)(2,1)S(1)}, u32[]{:S(2)}, u32[]{:S(2)}) collective-permute-start(bf16[512,512]{1,0:T(8,128)(2,1)S(1)} %fusion.16), channel_id=1, source_target_pairs={{0,1},{1,0},{2,3},{3,2},{4,5},{5,4},{6,7},{7,6},{8,9},{9,8},{10,11... | collective-permute-start | bytes 1572872 | tf_op jit(solution)/shard_map/ppermute | solution.py:326
  285.4 25.4 %collective-permute-start.5 = (bf16[1024,512]{1,0:T(8,128)(2,1)}, bf16[1024,512]{1,0:T(8,128)(2,1)S(1)}, u32[]{:S(2)}, u32[]{:S(2)}) collective-permute-start(bf16[1024,512]{1,0:T(8,128)(2,1)} %collective-permute-done.3), channel_id=1, source_target_pairs={{0,8},{8,0},{16,24},{24,16},{1,9},{9,1},{17,25},{25,17},{2,10},{10... | collective-permute-start | bytes 3145736 | tf_op jit(solution)/shard_map/ppermute | solution.py:307
  286.0 25.5 %collective-permute-start.4 = (bf16[1024,512]{1,0:T(8,128)(2,1)}, bf16[1024,512]{1,0:T(8,128)(2,1)S(1)}, u32[]{:S(2)}, u32[]{:S(2)}) collective-permute-start(bf16[1024,512]{1,0:T(8,128)(2,1)} %collective-permute-done), channel_id=1, source_target_pairs={{0,16},{8,24},{16,0},{24,8},{1,17},{9,25},{17,1},{25,9},{2,18},{10... | collective-permute-start | bytes 3145736 | tf_op jit(solution)/shard_map/ppermute | solution.py:306
  288.5 3.1 copy-start.5
  310.8 2.3 copy-start.18
  311.5 1.6 copy-start.16
  313.1 7.8 %collective-permute-start.9 = (bf16[512,512]{1,0:T(8,128)(2,1)}, bf16[512,512]{1,0:T(8,128)(2,1)}, u32[]{:S(2)}, u32[]{:S(2)}) collective-permute-start(bf16[512,512]{1,0:T(8,128)(2,1)} %fusion.17), channel_id=1, source_target_pairs={{0,1},{1,0},{2,3},{3,2},{4,5},{5,4},{6,7},{7,6},{8,9},{9,8},{10,11... | collective-permute-start | bytes 1572872 | tf_op jit(solution)/shard_map/ppermute | solution.py:326
  314.9 5.2 %copy-start.8 = (bf16[2,512,512]{2,1,0:T(8,128)(2,1)S(1)}, bf16[2,512,512]{2,1,0:T(8,128)(2,1)}, u32[]{:S(2)}) copy-start(bf16[2,512,512]{2,1,0:T(8,128)(2,1)} %get-tuple-element.31) | copy-start | bytes 3145732
  314.9 5.2 %copy-start.19 = (bf16[1024,512]{1,0:T(8,128)(2,1)S(1)}, bf16[1024,512]{1,0:T(8,128)(2,1)}, u32[]{:S(2)}) copy-start(bf16[1024,512]{1,0:T(8,128)(2,1)} %copy-done.18) | copy-start | bytes 3145732
  320.1 1.2 copy-start.17
  320.9 2.3 copy-start.13
  320.9 2.3 copy-start.14
  320.9 2.3 copy-start.15
  323.2 6.7 %copy-start.1 = (bf16[768,768]{1,0:T(8,128)(2,1)S(1)}, bf16[768,768]{1,0:T(8,128)(2,1)}, u32[]{:S(2)}) copy-start(bf16[768,768]{1,0:T(8,128)(2,1)} %param.16) | copy-start | bytes 3538948
Sparse Core Ops, SparseCore 0:
  214.5 57.4 all-reduce.4
where the time goes:
time: 338 us; the launch traced here: 337 us
  waiting for transfers between devices  109 us (32%)
  Pallas kernels  59.4 us (18%)
  blocking collectives  41.8 us (12%)
  local copies, waits for them, and re-layouts  39.5 us (12%)
  matrix products  35.2 us (10%)
  starting transfers between devices  20.7 us (6%)
  other arithmetic  16.5 us (5%)
  between operations  14.5 us (4%)
    psum x1, waiting for transfers between devices, on_device(): lax.psum(ret_part_grad.astype(jnp.bfloat16), ('enc', 'ret'))  51.5 us
    psum x1, blocking collectives, on_device(): lax.psum((mass_part, score_part.reshape(question_count, PASS)), ('enc', '...  41.8 us
    pallas_call x1, Pallas kernels, project(): pl.pallas_call(functools.partial(project_kernel, heads_here), grid=(width...  39.6 us
    dot_general x17, matrix products, wedge(): lax.dot_general(left, right, (((0,), (0,)), ((), ())), preferred_element_...  31.4 us
    all_to_all x1, waiting for transfers between devices, on_device(): kv = lax.all_to_all(sent, 'enc', split_axis=0, concat_axis=0, tiled=True)  23.7 us
    all_to_all x2, waiting for transfers between devices, columns_of(): lax.all_to_all(block, 'enc', split_axis=0, concat_axis=0, tiled=True)  20.2 us
    dynamic_slice x3, local copies, waits for them, and re-layouts, columns_of(): block = lax.dynamic_index_in_dim(split_cols, rank, axis=2, keepdims=False)  18.3 us
    ppermute x1, waiting for transfers between devices, on_device(): three_bottom = lax.ppermute(two_bottom, 'enc', flip[0])  13.6 us
  transfers between devices with their start and end apart: 14, of which 4 were waited for; matrix products, arithmetic and copies ran while one was open for 17% of the time, Pallas kernels for 13%

commit v1 on v0

--- a/solution.py
+++ b/solution.py
@@ -183,6 +183,19 @@
     return lax.dot_general(
         left, right, (((0,), (0,)), ((), ())), preferred_element_type=jnp.float32
     )
+
+
+def sum_over(value, axes):
+    for axis in axes:
+        size = lax.axis_size(axis)
+        if size & (size - 1):
+            value = lax.psum(value, axis)
+            continue
+        bit = 1
+        while bit < size:
+            value = value + lax.ppermute(value, axis, [(i, i ^ bit) for i in range(size)])
+            bit *= 2
+    return value
 
 
 def on_device(
@@ -220,11 +233,17 @@
 
     rows_out = width // (n_enc * n_ret)
     rows_group = group_pass * slot_len
-    split_cols = tok_rows.reshape(rows_dev, n_enc, n_ret, rows_out)
 
     def columns_of(rank):
-        block = lax.dynamic_index_in_dim(split_cols, rank, axis=2, keepdims=False)
-        block = jnp.transpose(block, (1, 0, 2))
+        blocks = []
+        for j in range(n_enc):
+            first = j * n_ret * rows_out
+            block = tok_rows[:, first : first + rows_out]
+            for k in range(1, n_ret):
+                start = first + k * rows_out
+                block = jnp.where(rank == k, tok_rows[:, start : start + rows_out], block)
+            blocks.append(block)
+        block = jnp.stack(blocks)
         return lax.all_to_all(block, "enc", split_axis=0, concat_axis=0, tiled=True).reshape(
             rows_group, rows_out
         )
@@ -288,8 +307,8 @@
     slot_embed = jnp.dot(owner_map, embed_own, precision=highest)
     emb_rep = jnp.repeat(question_emb, PASS, axis=0)
     score_part = jnp.sum(emb_rep * slot_embed, axis=-1) * (dec_rank == 0).astype(jnp.float32)
-    passage_mass, ret_scores = lax.psum(
-        (mass_part, score_part.reshape(question_count, PASS)), ("enc", "dec")
+    passage_mass, ret_scores = sum_over(
+        jnp.stack([mass_part, score_part.reshape(question_count, PASS)]), ("enc", "dec")
     )
     own_grad, passage_mass, ret_scores = lax.optimization_barrier(
         (own_grad, passage_mass, ret_scores)

time: 338 us -> 284 us (0.84)
  blocking collectives: 41.8 us -> 0 us
  local copies, waits for them, and re-layouts: 39.5 us -> 12.2 us
  starting transfers between devices: 20.7 us -> 28.4 us
  other arithmetic: 16.5 us -> 22.4 us
    psum x1 -> x0, blocking collectives: 41.8 us -> none  [on_device(): lax.psum((mass_part, score_part.reshape(question_count, PASS)), ('enc', '...]
    all_to_all x2, waiting for transfers between devices: 20.2 us -> 0.01 us  [columns_of(): lax.all_to_all(block, 'enc', split_axis=0, concat_axis=0, tiled=True)]
    dynamic_slice x3 -> x0, local copies, waits for them, and re-layouts: 18.3 us -> none  [columns_of(): block = lax.dynamic_index_in_dim(split_cols, rank, axis=2, keepdims=False)]
    ppermute x0 -> x4, waiting for transfers between devices: none -> 10.4 us  [sum_over(): lax.ppermute(value, axis, [(i, i ^ bit) for i in range(size)])]
    another operation x1, local copies, waits for them, and re-layouts: 7.89 us -> 0.01 us  [on_device(): passage_mass, ret_scores = sum_over(jnp.stack([mass_part, score_part.resh...]
    ppermute x0 -> x4, starting transfers between devices: none -> 7.83 us  [sum_over(): lax.ppermute(value, axis, [(i, i ^ bit) for i in range(size)])]
    another operation x0 -> x4, other arithmetic: none -> 6.88 us  [the longest x3 6.87 us: columns_of(): block = jnp.stack(blocks)]
    all_to_all x1, waiting for transfers between devices: 23.7 us -> 30.5 us  [on_device(): kv = lax.all_to_all(sent, 'enc', split_axis=0, concat_axis=0, tiled=True)]
  transfers between devices with their start and end apart: 14 -> 18, of which waited for: 4 -> 6; matrix products, arithmetic and copies ran while one was open for 17% -> 20% of each run, Pallas kernels for 13% -> 19%
where the time goes in v1:
time: 284 us; the launch traced here: 282 us
  waiting for transfers between devices  109 us (38%)
  Pallas kernels  59.5 us (21%)
  matrix products  35.9 us (13%)
  starting transfers between devices  28.4 us (10%)
  other arithmetic  22.4 us (8%)
  between operations  14.5 us (5%)
  local copies, waits for them, and re-layouts  12.2 us (4%)
    psum x1, waiting for transfers between devices, on_device(): lax.psum(ret_part_grad.astype(jnp.bfloat16), ('enc', 'ret'))  54.9 us
    pallas_call x1, Pallas kernels, project(): pl.pallas_call(functools.partial(project_kernel, heads_here), grid=(width...  39.7 us
    dot_general x17, matrix products, wedge(): lax.dot_general(left, right, (((0,), (0,)), ((), ())), preferred_element_...  31.9 us
    all_to_all x1, waiting for transfers between devices, on_device(): kv = lax.all_to_all(sent, 'enc', split_axis=0, concat_axis=0, tiled=True)  30.5 us
    ppermute x1, waiting for transfers between devices, on_device(): three_bottom = lax.ppermute(two_bottom, 'enc', flip[0])  13.7 us
    ppermute x4, waiting for transfers between devices, sum_over(): lax.ppermute(value, axis, [(i, i ^ bit) for i in range(size)])  10.4 us
    pallas_call x2, Pallas kernels, spread(): pl.pallas_call(spread_kernel, grid_spec=pltpu.PrefetchScalarGridSpec(num_...  10.2 us
    all_to_all x2, starting transfers between devices, columns_of(): lax.all_to_all(block, 'enc', split_axis=0, concat_axis=0, tiled=True)  9.63 us
  transfers between devices with their start and end apart: 18, of which 6 were waited for; matrix products, arithmetic and copies ran while one was open for 20% of the time, Pallas kernels for 19%

profile of v1, /device:TPU:0, one launch (start us, length us, event | category | flops | bytes accessed | tf_op | source)
XLA Modules:
  0.0 282.5 jit_solution(2262248601822104667)
XLA Ops:
  7.2 3.7 %select_bitcast_fusion.3 = (bf16[1,512,512]{2,1,0:T(8,128)(2,1)S(1)}, bf16[1,512,512]{2,1,0:T(8,128)(2,1)}, bf16[1,512,512]{2,1,0:T(8,128)(2,1)}, bf16[1,512,512...) fusion(pred[]{:T(512)S(6)} %eq.38, ...), kind=kLoop, calls=%fused_computation.56 | loop fusion | flops 2097152 | bytes 8388610 | tf_op jit(solution)/shard_map/stack | solution.py:246
  10.9 1.6 pad_maximum_fusion.2
  12.5 5.2 %all-to-all-start.2 = ((bf16[4,512,512]{2,1,0:T(8,128)(2,1)}), bf16[4,512,512]{2,1,0:T(8,128)(2,1)S(1)}, u32[]{:S(2)}, u32[]{:S(2)}) async-start(bf16[4,512,512]{2,1,0:T(8,128)(2,1)} %pad_maximum_fusion.2), calls=%async_computation.2 | async-start | bytes 4194304 | tf_op jit(solution)/shard_map/all_to_all | solution.py:247
  17.7 39.7 %project.1 = bf16[4,512,768]{2,1,0:T(8,128)(2,1)} custom-call(bf16[512,4096]{1,0:T(8,128)(2,1)} %bitcast.108, bf16[4096,16,128]{2,1,0:T(8,128)(2,1)} %w_ref.1), custom_call_target="tpu_custom_call" | custom-call | flops 8589934592 | bytes 24117248 | tf_op jit(solution)/shard_map/project/pallas_call | solution.py:63
  57.4 4.8 %all-to-all-start = ((bf16[4,512,768]{2,1,0:T(8,128)(2,1)}), bf16[4,512,768]{2,1,0:T(8,128)(2,1)}, u32[]{:S(2)}, u32[]{:S(2)}) async-start(bf16[4,512,768]{2,1,0:T(8,128)(2,1)} %project.1), calls=%async_computation | async-start | bytes 6291456 | tf_op jit(solution)/shard_map/all_to_all | solution.py:254
  62.5 3.4 %select_reduce_fusion = (f32[2,768]{1,0:T(2,128)S(1)}, f32[2,256,768]{2,1,0:T(8,128)}) fusion(pred[2,256]{1,0:T(4,128)(4,1)S(1)} %iota_compare_fusion.3, bf16[768,768]{1,0:T(8,128)(2,1)S(1)} %copy-done, bf16[2,1,256,768]{3,2,1,0:T(8,128)(2,1)} %param.15), kind=kOutput, calls=%fused_computation.19 | convolution fusion | flops 607910400 | bytes 3545600 | tf_op jit(solution)/shard_map/dot_general | solution.py:297
  66.2 1.6 pad_maximum_fusion.1
  67.9 30.5 %all-to-all-done = bf16[4,512,768]{2,1,0:T(8,128)(2,1)} async-done(((bf16[4,512,768]{2,1,0:T(8,128)(2,1)}), bf16[4,512,768]{2,1,0:T(8,128)(2,1)}, u32[]{:S(2)}, u32[]{:S(2)}) %all-to-all-start) | async-done | bytes 3145760 | tf_op jit(solution)/shard_map/all_to_all | solution.py:254
  98.4 4.4 %all-to-all-start.1 = ((bf16[4,512,512]{2,1,0:T(8,128)(2,1)}), bf16[4,512,512]{2,1,0:T(8,128)(2,1)}, u32[]{:S(2)}, u32[]{:S(2)}) async-start(bf16[4,512,512]{2,1,0:T(8,128)(2,1)} %pad_maximum_fusion.1), calls=%async_computation.1 | async-start | bytes 4194304 | tf_op jit(solution)/shard_map/all_to_all | solution.py:247
  105.2 9.6 %attend.1 = (bf16[1,2048,512]{2,1,0:T(8,128)(2,1)}, f32[1,1,2048]{2,1,0:T(1,128)}) custom-call(bf16[1,4,256,128]{3,2,1,0:T(8,128)(2,1)} %fusion.31.x_ref, bf16[1,2048,768]{2,1,0:T(8,128)(2,1)} %bitcast.3.kv_ref, f32[1,1,2048]{2,1,0:T(1,128)} %reshape.181.live_ref), custom_call_target="tpu_custom_call" | custom-call | flops 1342177280 | bytes 5242880 | tf_op jit(solution)/shard_map/attend/pallas_call | solution.py:123
  115.3 1.4 reduce.7
  117.5 1.8 collective-permute-start
  119.3 8.0 %collective-permute-done = f32[2,1,8]{2,1,0:T(1,128)S(1)} collective-permute-done((f32[2,1,8]{2,1,0:T(1,128)S(1)}, f32[2,1,8]{2,1,0:T(1,128)S(1)}, u32[]{:S(2)}, u32[]{:S(2)}) %collective-permute-start) | collective-permute-done | bytes 96 | tf_op jit(solution)/shard_map/ppermute | solution.py:196
  127.3 1.5 collective-permute-start.1
  128.7 2.1 collective-permute-done.1
  130.8 1.8 collective-permute-start.2
  132.6 1.5 fusion.60
  134.4 2.8 collective-permute-start.3
  137.2 2.7 fusion.61
  140.0 2.1 fusion.62
  142.3 1.7 collective-permute-start.7
  144.0 1.6 collective-permute-start.4
  147.4 1.5 fusion.14
  149.5 1.3 fusion.48
  152.3 2.6 fusion.6
  154.9 1.8 fusion.10
  156.8 2.1 fusion.56
  160.1 1.8 fusion.28
  161.9 54.9 %all-reduce.4.cloned.1.call-done = bf16[768,768]{0,1:T(8,128)(2,1)} async-done(((bf16[768,768]{0,1:T(8,128)(2,1)}), bf16[768,768]{0,1:T(8,128)(2,1)}) %all-reduce.4.cloned.1.call-update) | async-done | bytes 1179664 | tf_op jit(solution)/shard_map/psum | solution.py:372
  216.8 2.4 copy.19
  219.2 2.4 fusion.64
  221.6 2.0 fusion.15
  223.7 2.0 fusion.66
  225.7 2.0 fusion.16
  228.3 2.0 fusion.63
  231.4 2.0 fusion.65
  233.4 1.6 select_bitcast_fusion.10
  235.0 1.5 select_bitcast_fusion.9
  236.5 2.8 fusion.23
  239.2 2.7 fusion.22
  242.0 13.7 %collective-permute-done.9 = bf16[1024,512]{1,0:T(8,128)(2,1)S(1)} collective-permute-done((bf16[1024,512]{1,0:T(8,128)(2,1)}, bf16[1024,512]{1,0:T(8,128)(2,1)S(1)}, u32[]{:S(2)}, u32[]{:S(2)}) %collective-permute-start.9) | collective-permute-done | bytes 1048608 | tf_op jit(solution)/shard_map/ppermute | solution.py:326
  256.4 1.6 fusion.17
  258.2 1.6 pad_maximum_fusion.piece_ref
  259.8 5.2 %spread.2 = bf16[512,16,128]{2,1,0:T(8,128)(2,1)} custom-call(s32[4]{0:T(128)} %iota_xor_fusion.where_ref, bf16[4,512,512]{2,1,0:T(8,128)(2,1)} %pad_maximum_fusion.piece_ref), custom_call_target="tpu_custom_call" | custom-call | bytes 4194304 | tf_op jit(solution)/shard_map/spread/pallas_call | solution.py:165
  265.0 2.0 fusion.67
  267.1 1.9 fusion.21
  269.0 1.6 pad_maximum_fusion.3.piece_ref
  270.6 5.0 %spread.3 = bf16[512,16,128]{2,1,0:T(8,128)(2,1)} custom-call(s32[4]{0:T(128)} %iota_xor_fusion.where_ref, bf16[4,512,512]{2,1,0:T(8,128)(2,1)} %pad_maximum_fusion.3.piece_ref), custom_call_target="tpu_custom_call" | custom-call | bytes 4194304 | tf_op jit(solution)/shard_map/spread/pallas_call | solution.py:165
  (112 shorter events, 12.9 us)
Async XLA Ops:
  7.2 55.3 %copy-start = (bf16[768,768]{1,0:T(8,128)(2,1)S(1)}, bf16[768,768]{1,0:T(8,128)(2,1)}, u32[]{:S(2)}) copy-start(bf16[768,768]{1,0:T(8,128)(2,1)} %param.16) | copy-start | bytes 3538948
  12.5 44.9 %all-to-all-start.2 = ((bf16[4,512,512]{2,1,0:T(8,128)(2,1)}), bf16[4,512,512]{2,1,0:T(8,128)(2,1)S(1)}, u32[]{:S(2)}, u32[]{:S(2)}) async-start(bf16[4,512,512]{2,1,0:T(8,128)(2,1)} %pad_maximum_fusion.2), calls=%async_computation.2 | async-start | bytes 4194304 | tf_op jit(solution)/shard_map/all_to_all | solution.py:247
  57.3 4.9 %copy-start.24 = (f32[1,768]{1,0:T(1,128)S(1)}, f32[1,768]{1,0:T(1,128)}, u32[]{:S(2)}) copy-start(f32[1,768]{1,0:T(1,128)} %param.17) | copy-start | bytes 9220
  57.3 4.9 %copy-start.25 = (s32[1,8]{1,0:T(1,128)S(1)}, s32[1,8]{1,0:T(1,128)}, u32[]{:S(2)}) copy-start(s32[1,8]{1,0:T(1,128)} %param.14) | copy-start | bytes 100
  57.3 5.0 %copy-start.27 = (s32[1,8]{1,0:T(1,128)S(1)}, s32[1,8]{1,0:T(1,128)}, u32[]{:S(2)}) copy-start(s32[1,8]{1,0:T(1,128)} %param.13) | copy-start | bytes 100
  57.4 41.0 %all-to-all-start = ((bf16[4,512,768]{2,1,0:T(8,128)(2,1)}), bf16[4,512,768]{2,1,0:T(8,128)(2,1)}, u32[]{:S(2)}, u32[]{:S(2)}) async-start(bf16[4,512,768]{2,1,0:T(8,128)(2,1)} %project.1), calls=%async_computation | async-start | bytes 6291456 | tf_op jit(solution)/shard_map/all_to_all | solution.py:254
  62.4 3.7 %copy-start.4 = (bf16[1,512,512]{2,1,0:T(8,128)(2,1)S(1)}, bf16[1,512,512]{2,1,0:T(8,128)(2,1)}, u32[]{:S(2)}) copy-start(bf16[1,512,512]{2,1,0:T(8,128)(2,1)} %get-tuple-element.22) | copy-start | bytes 1572868
  62.4 3.7 %copy-start.5 = (bf16[1,512,512]{2,1,0:T(8,128)(2,1)S(1)}, bf16[1,512,512]{2,1,0:T(8,128)(2,1)}, u32[]{:S(2)}) copy-start(bf16[1,512,512]{2,1,0:T(8,128)(2,1)} %get-tuple-element.23) | copy-start | bytes 1572868
  62.4 3.8 %copy-start.6 = (bf16[1,512,512]{2,1,0:T(8,128)(2,1)S(1)}, bf16[1,512,512]{2,1,0:T(8,128)(2,1)}, u32[]{:S(2)}) copy-start(bf16[1,512,512]{2,1,0:T(8,128)(2,1)} %get-tuple-element.24) | copy-start | bytes 1572868
  62.4 3.8 %copy-start.7 = (bf16[1,512,512]{2,1,0:T(8,128)(2,1)S(1)}, bf16[1,512,512]{2,1,0:T(8,128)(2,1)}, u32[]{:S(2)}) copy-start(bf16[1,512,512]{2,1,0:T(8,128)(2,1)} %get-tuple-element.25) | copy-start | bytes 1572868
  67.9 35.7 %copy-start.22 = (bf16[1,128,4,64]{1,3,2,0:T(8,128)(2,1)S(1)}, bf16[1,128,4,64]{1,3,2,0:T(8,128)(2,1)}, u32[]{:S(2)}) copy-start(bf16[1,128,4,64]{1,3,2,0:T(8,128)(2,1)} %param.11) | copy-start | bytes 196612
  67.9 35.8 %copy-start.23 = (bf16[1,128,4,64]{1,3,2,0:T(8,128)(2,1)S(1)}, bf16[1,128,4,64]{1,3,2,0:T(8,128)(2,1)}, u32[]{:S(2)}) copy-start(bf16[1,128,4,64]{1,3,2,0:T(8,128)(2,1)} %param.12) | copy-start | bytes 196612
  98.4 38.9 %all-to-all-start.1 = ((bf16[4,512,512]{2,1,0:T(8,128)(2,1)}), bf16[4,512,512]{2,1,0:T(8,128)(2,1)}, u32[]{:S(2)}, u32[]{:S(2)}) async-start(bf16[4,512,512]{2,1,0:T(8,128)(2,1)} %pad_maximum_fusion.1), calls=%async_computation.1 | async-start | bytes 4194304 | tf_op jit(solution)/shard_map/all_to_all | solution.py:247
  102.8 114.0 %all-reduce.4.cloned.1.call-start = ((), (), s32[]{:S(2)}) async-start(), calls=%async_computation.3 | async-start | bytes 2359296 | tf_op jit(solution)/shard_map/psum | solution.py:372
  117.5 9.8 %collective-permute-start = (f32[2,1,8]{2,1,0:T(1,128)S(1)}, f32[2,1,8]{2,1,0:T(1,128)S(1)}, u32[]{:S(2)}, u32[]{:S(2)}) collective-permute-start(f32[2,1,8]{2,1,0:T(1,128)S(1)} %pad_maximum_fusion.4), channel_id=1, source_target_pairs={{0,8},{8,0},{16,24},{24,16},{1,9},{9,1},{17,25},{25,17},{2,10},{10... | collective-permute-start | bytes 200 | tf_op jit(solution)/shard_map/ppermute | solution.py:196
  127.3 3.6 %collective-permute-start.1 = (f32[2,1,8]{2,1,0:T(1,128)S(1)}, f32[2,1,8]{2,1,0:T(1,128)S(1)}, u32[]{:S(2)}, u32[]{:S(2)}) collective-permute-start(f32[2,1,8]{2,1,0:T(1,128)S(1)} %fusion.49), channel_id=1, source_target_pairs={{0,16},{8,24},{16,0},{24,8},{1,17},{9,25},{17,1},{25,9},{2,18},{10... | collective-permute-start | bytes 200 | tf_op jit(solution)/shard_map/ppermute | solution.py:196
  130.8 3.6 %collective-permute-start.2 = (f32[2,1,8]{2,1,0:T(1,128)S(1)}, f32[2,1,8]{2,1,0:T(1,128)S(1)}, u32[]{:S(2)}, u32[]{:S(2)}) collective-permute-start(f32[2,1,8]{2,1,0:T(1,128)S(1)} %fusion.99), channel_id=1, source_target_pairs={{0,2},{2,0},{4,6},{6,4},{1,3},{3,1},{5,7},{7,5},{8,10},{10,8},{12,... | collective-permute-start | bytes 200 | tf_op jit(solution)/shard_map/ppermute | solution.py:196
  134.4 5.5 %collective-permute-start.3 = (f32[2,1,8]{2,1,0:T(1,128)S(1)}, f32[2,1,8]{2,1,0:T(1,128)S(1)}, u32[]{:S(2)}, u32[]{:S(2)}) collective-permute-start(f32[2,1,8]{2,1,0:T(1,128)S(1)} %add.113), channel_id=1, source_target_pairs={{0,4},{2,6},{4,0},{6,2},{1,5},{3,7},{5,1},{7,3},{8,12},{10,14},{12... | collective-permute-start | bytes 200 | tf_op jit(solution)/shard_map/ppermute | solution.py:196
  139.9 16.8 %copy-start.8 = (bf16[2,512,512]{2,1,0:T(8,128)(2,1)}, bf16[2,512,512]{2,1,0:T(8,128)(2,1)S(1)}, u32[]{:S(2)}) copy-start(bf16[2,512,512]{2,1,0:T(8,128)(2,1)S(1)} %get-tuple-element.31) | copy-start | bytes 3145732
  139.9 6.2 %copy-start.2 = (bf16[1,2048,512]{2,1,0:T(8,128)(2,1)S(1)}, bf16[1,2048,512]{2,1,0:T(8,128)(2,1)}, u32[]{:S(2)}) copy-start(bf16[1,2048,512]{2,1,0:T(8,128)(2,1)} %get-tuple-element.8) | copy-start | bytes 6291460
  140.0 6.2 %copy-start.10 = (bf16[2,512,512]{2,1,0:T(8,128)(2,1)S(1)}, bf16[2,512,512]{2,1,0:T(8,128)(2,1)}, u32[]{:S(2)}) copy-start(bf16[2,512,512]{2,1,0:T(8,128)(2,1)} %get-tuple-element.29) | copy-start | bytes 3145732
  142.1 77.1 %collective-permute-start.5 = (bf16[1024,512]{1,0:T(8,128)(2,1)S(1)}, bf16[1024,512]{1,0:T(8,128)(2,1)}, u32[]{:S(2)}, u32[]{:S(2)}) collective-permute-start(bf16[1024,512]{1,0:T(8,128)(2,1)S(1)} %get-tuple-element.34), channel_id=1, source_target_pairs={{0,8},{8,0},{16,24},{24,16},{1,9},{9,1},{17,25},{25,17},{2,10},{10... | collective-permute-start | bytes 3145736 | tf_op jit(solution)/shard_map/ppermute | solution.py:323
  142.3 81.4 %collective-permute-start.7 = (bf16[1024,512]{1,0:T(8,128)(2,1)S(1)}, bf16[1024,512]{1,0:T(8,128)(2,1)}, u32[]{:S(2)}, u32[]{:S(2)}) collective-permute-start(bf16[1024,512]{1,0:T(8,128)(2,1)S(1)} %get-tuple-element.34), channel_id=1, source_target_pairs={{0,16},{8,24},{16,0},{24,8},{1,17},{9,25},{17,1},{25,9},{2,18},{10... | collective-permute-start | bytes 3145736 | tf_op jit(solution)/shard_map/ppermute | solution.py:322
  144.0 77.6 %collective-permute-start.4 = (bf16[1024,512]{1,0:T(8,128)(2,1)S(1)}, bf16[1024,512]{1,0:T(8,128)(2,1)}, u32[]{:S(2)}, u32[]{:S(2)}) collective-permute-start(bf16[1024,512]{1,0:T(8,128)(2,1)S(1)} %get-tuple-element.33), channel_id=1, source_target_pairs={{0,8},{8,0},{16,24},{24,16},{1,9},{9,1},{17,25},{25,17},{2,10},{10... | collective-permute-start | bytes 3145736 | tf_op jit(solution)/shard_map/ppermute | solution.py:321
  145.6 80.1 %collective-permute-start.6 = (bf16[1024,512]{1,0:T(8,128)(2,1)S(1)}, bf16[1024,512]{1,0:T(8,128)(2,1)}, u32[]{:S(2)}, u32[]{:S(2)}) collective-permute-start(bf16[1024,512]{1,0:T(8,128)(2,1)S(1)} %get-tuple-element.33), channel_id=1, source_target_pairs={{0,16},{8,24},{16,0},{24,8},{1,17},{9,25},{17,1},{25,9},{2,18},{10... | collective-permute-start | bytes 3145736 | tf_op jit(solution)/shard_map/ppermute | solution.py:324
  146.2 1.2 copy-start.15
  148.9 10.2 %collective-permute-start.10 = (bf16[512,512]{1,0:T(8,128)(2,1)}, bf16[512,512]{1,0:T(8,128)(2,1)}, u32[]{:S(2)}, u32[]{:S(2)}) collective-permute-start(bf16[512,512]{1,0:T(8,128)(2,1)} %fusion.14), channel_id=1, source_target_pairs={{0,1},{1,0},{2,3},{3,2},{4,5},{5,4},{6,7},{7,6},{8,9},{9,8},{10,11... | collective-permute-start | bytes 1572872 | tf_op jit(solution)/shard_map/ppermute | solution.py:345
  149.5 5.4 %copy-start.26 = (bf16[2,1,256,768]{3,2,1,0:T(8,128)(2,1)S(1)}, bf16[2,1,256,768]{3,2,1,0:T(8,128)(2,1)}, u32[]{:S(2)}) copy-start(bf16[2,1,256,768]{3,2,1,0:T(8,128)(2,1)} %param.15) | copy-start | bytes 2359300
  156.8 2.4 copy-start.3
  158.9 1.2 copy-start.12
  219.2 2.4 copy-start.11
  221.5 2.2 copy-start.16
  223.6 12.8 %collective-permute-start.11 = (bf16[512,512]{1,0:T(8,128)(2,1)S(1)}, bf16[512,512]{1,0:T(8,128)(2,1)S(1)}, u32[]{:S(2)}, u32[]{:S(2)}) collective-permute-start(bf16[512,512]{1,0:T(8,128)(2,1)S(1)} %fusion.15), channel_id=1, source_target_pairs={{0,1},{1,0},{2,3},{3,2},{4,5},{5,4},{6,7},{7,6},{8,9},{9,8},{10,11... | collective-permute-start | bytes 1572872 | tf_op jit(solution)/shard_map/ppermute | solution.py:345
  225.7 2.6 copy-start.13
  227.7 11.5 %collective-permute-start.12 = (bf16[512,512]{1,0:T(8,128)(2,1)S(1)}, bf16[512,512]{1,0:T(8,128)(2,1)S(1)}, u32[]{:S(2)}, u32[]{:S(2)}) collective-permute-start(bf16[512,512]{1,0:T(8,128)(2,1)S(1)} %fusion.16), channel_id=1, source_target_pairs={{0,1},{1,0},{2,3},{3,2},{4,5},{5,4},{6,7},{7,6},{8,9},{9,8},{10,11... | collective-permute-start | bytes 1572872 | tf_op jit(solution)/shard_map/ppermute | solution.py:345
  230.3 25.4 %collective-permute-start.9 = (bf16[1024,512]{1,0:T(8,128)(2,1)}, bf16[1024,512]{1,0:T(8,128)(2,1)S(1)}, u32[]{:S(2)}, u32[]{:S(2)}) collective-permute-start(bf16[1024,512]{1,0:T(8,128)(2,1)} %collective-permute-done.7), channel_id=1, source_target_pairs={{0,8},{8,0},{16,24},{24,16},{1,9},{9,1},{17,25},{25,17},{2,10},{10... | collective-permute-start | bytes 3145736 | tf_op jit(solution)/shard_map/ppermute | solution.py:326
  230.9 25.5 %collective-permute-start.8 = (bf16[1024,512]{1,0:T(8,128)(2,1)}, bf16[1024,512]{1,0:T(8,128)(2,1)S(1)}, u32[]{:S(2)}, u32[]{:S(2)}) collective-permute-start(bf16[1024,512]{1,0:T(8,128)(2,1)} %collective-permute-done.4), channel_id=1, source_target_pairs={{0,16},{8,24},{16,0},{24,8},{1,17},{9,25},{17,1},{25,9},{2,18},{10... | collective-permute-start | bytes 3145736 | tf_op jit(solution)/shard_map/ppermute | solution.py:325
  233.4 3.1 %copy-start.9 = (bf16[2,512,512]{2,1,0:T(8,128)(2,1)S(1)}, bf16[2,512,512]{2,1,0:T(8,128)(2,1)}, u32[]{:S(2)}) copy-start(bf16[2,512,512]{2,1,0:T(8,128)(2,1)} %copy-done.8) | copy-start | bytes 3145732
  255.6 2.3 copy-start.21
  256.4 1.6 copy-start.19
  257.9 9.1 %collective-permute-start.13 = (bf16[512,512]{1,0:T(8,128)(2,1)}, bf16[512,512]{1,0:T(8,128)(2,1)}, u32[]{:S(2)}, u32[]{:S(2)}) collective-permute-start(bf16[512,512]{1,0:T(8,128)(2,1)} %fusion.17), channel_id=1, source_target_pairs={{0,1},{1,0},{2,3},{3,2},{4,5},{5,4},{6,7},{7,6},{8,9},{9,8},{10,11... | collective-permute-start | bytes 1572872 | tf_op jit(solution)/shard_map/ppermute | solution.py:345
  259.8 5.2 %copy-start.14 = (bf16[2,512,512]{2,1,0:T(8,128)(2,1)S(1)}, bf16[2,512,512]{2,1,0:T(8,128)(2,1)}, u32[]{:S(2)}) copy-start(bf16[2,512,512]{2,1,0:T(8,128)(2,1)} %get-tuple-element.32) | copy-start | bytes 3145732
  265.0 2.1 copy-start.20
  267.0 1.9 copy-start.17
  267.0 1.9 copy-start.18
  269.0 6.7 %copy-start.1 = (bf16[768,768]{1,0:T(8,128)(2,1)S(1)}, bf16[768,768]{1,0:T(8,128)(2,1)}, u32[]{:S(2)}) copy-start(bf16[768,768]{1,0:T(8,128)(2,1)} %param.16) | copy-start | bytes 3538948
Sparse Core Ops, SparseCore 0:
  156.9 59.8 all-reduce.3
